TPU v7x, 128 devices: a whole 4x4x4 slice. The times are simulated.
128 devices in a mesh: replica: 16 (over x_lo, z, core), tensor: 8 (over y, x_hi).
Axes of the slice: x: 4 (x_hi: 2, x_lo: 2; x = x_hi * 2 + x_lo), y: 4, z: 4, core: 2. Of those that a mesh axis runs over, the one named last changes fastest.
Arguments:
- tokens: bfloat16 [8192, 1024], P('replica'), may hold values from -6 to 6
- targets: bfloat16 [8192, 1024], P('replica'), may hold values from -6 to 6
- row_ids: int32 [16, 3, 512], P('replica'), may hold values from 0 to 511
- anchor: float32 [2, 1024, 4096], P(None, None, 'tensor'), may hold values from -0.1875 to 0.1875
- momentum: float32 [16, 2, 1024, 4096], P('replica', None, None, 'tensor'), may hold values from -4 to 4
- slow: float32 [2, 1024, 4096], P(None, None, 'tensor'), may hold values from -6 to 6
Outputs:
- anchor_new: float32 [2, 1024, 4096], P(None, None, 'tensor')
- slow_new: float32 [2, 1024, 4096], P(None, None, 'tensor')
- momentum_new: float32 [16, 2, 1024, 4096], P('replica', None, None, 'tensor')
Inputs may be any that keep to these rules, and one draw needn't show every extreme that they name: `row_ids`: each id names a row within its replica's own block of 512 rows; rows may repeat.
All inputs are finite; a program needn't handle non-finite values.
Results may differ from a plain program's by a relative error of at most 0.008.
Values may be sent and summed in bfloat16 or wider, within the bound.
A program may use at most 128 MiB of HBM per device.

v0:
```python
import jax
import jax.numpy as jnp
from jax import lax
from jax.sharding import PartitionSpec as P

INNER = 3
learn_rate = 0.02
inner_beta = 0.9
slow_beta = 0.5


def passed_along(block, axis, distance):
    devices = range(lax.axis_size(axis))
    route = [((i - distance) % len(devices), i) for i in devices]
    return lax.ppermute(block, axis, route)


def gelu_pair(pre):
    coeff = 0.7978845608028654
    inner = coeff * (pre + 0.044715 * pre * pre * pre)
    tanh_val = jnp.tanh(inner)
    value = 0.5 * pre * (1.0 + tanh_val)
    slope = 0.5 * (1.0 + tanh_val) + 0.5 * pre * (1.0 - tanh_val * tanh_val) * coeff * (
        1.0 + 3.0 * 0.044715 * pre * pre
    )
    return (value, slope)


def body(tokens, targets, row_ids, anchor, momentum, slow):
    row_count = tokens.shape[0]
    scale = 1.0 / row_count
    weights = anchor
    moment = momentum[0]
    parts = lax.axis_size("tensor")
    own = lax.axis_index("tensor")
    shard_rows = row_count // parts
    for step in range(INNER):
        if step > 0:
            incoming = passed_along(weights.astype(jnp.bfloat16), "replica", 2 ** (step - 1))
            weights = 0.5 * (weights + incoming.astype(jnp.float32))
        picks = row_ids[0, step]
        inputs = jnp.take(tokens, picks, axis=0)
        own_picks = lax.dynamic_slice(picks, (own * shard_rows,), (shard_rows,))
        wanted = jnp.take(targets, own_picks, axis=0)
        weights_bf = weights.astype(jnp.bfloat16)
        pre = jnp.dot(inputs, weights_bf[0], preferred_element_type=jnp.float32)
        value, slope = gelu_pair(pre)
        hidden = value.astype(jnp.bfloat16)
        partial_out = lax.dot_general(
            hidden, weights_bf[1], (((1,), (1,)), ((), ())), preferred_element_type=jnp.float32
        ).astype(jnp.bfloat16)
        summed = lax.psum_scatter(partial_out, "tensor", scatter_dimension=0, tiled=True)
        error = ((summed.astype(jnp.float32) - wanted.astype(jnp.float32)) * scale).astype(
            jnp.bfloat16
        )
        error = lax.all_gather(error, "tensor", axis=0, tiled=True)
        back = (jnp.dot(error, weights_bf[1], preferred_element_type=jnp.float32) * slope).astype(
            jnp.bfloat16
        )
        grad_in = lax.dot_general(
            inputs, back, (((0,), (0,)), ((), ())), preferred_element_type=jnp.float32
        )
        grad_out = lax.dot_general(
            error, hidden, (((0,), (0,)), ((), ())), preferred_element_type=jnp.float32
        )
        moment = inner_beta * moment + jnp.stack([grad_in, grad_out])
        weights = weights - learn_rate * moment
    replicas = lax.axis_size("replica")
    moved = ((anchor - weights) / learn_rate).astype(jnp.bfloat16)
    total = lax.psum_scatter(moved, "replica", scatter_dimension=1, tiled=True)
    total = lax.all_gather(total, "replica", axis=1, tiled=True)
    slow_new = slow_beta * slow + total.astype(jnp.float32) / replicas
    anchor_new = anchor - learn_rate * slow_new
    return (anchor_new, slow_new, moment[None])


def solution(mesh):
    return jax.shard_map(
        body,
        mesh=mesh,
        in_specs=(
            P("replica", None),
            P("replica", None),
            P("replica", None, None),
            P(None, None, "tensor"),
            P("replica", None, None, "tensor"),
            P(None, None, "tensor"),
        ),
        out_specs=(
            P(None, None, "tensor"),
            P(None, None, "tensor"),
            P("replica", None, None, "tensor"),
        ),
        check_vma=False,
    )
```

profile of v0, /device:TPU:1, one launch (start us, length us, event | category | flops | bytes accessed | tf_op | source)
XLA Modules:
  0.0 628.3 jit_solution(16959371402139294303)
XLA Ops:
  7.2 0.8 fusion.106
  8.1 2.5 convert_element_type.81
  10.5 2.8 gather_fusion
  13.3 2.0 fusion.37
  15.3 1.0 copy-done.19
  16.3 3.1 convolution_convert_fusion.2
  19.6 0.7 gather_fusion.1
  20.3 72.9 %reduce-scatter.5.cloned.1.call-done = bf16[64,1024]{1,0:T(8,128)(2,1)} async-done(((bf16[512,1024]{1,0:T(8,128)(2,1)}), bf16[64,1024]{1,0:T(8,128)(2,1)}) %reduce-scatter.5.cloned.1.call-update) | async-done | bytes 131088 | tf_op jit(solution)/shard_map/reduce_scatter | solution.py:52
  93.2 1.7 multiply_convert_fusion.5
  95.0 46.8 %all-gather.5.cloned.1.call-done = bf16[512,1024]{1,0:T(8,128)(2,1)} async-done(((bf16[64,1024]{1,0:T(8,128)(2,1)}), bf16[512,1024]{1,0:T(8,128)(2,1)}) %all-gather.5.cloned.1.call-update) | async-done | bytes 1048592 | tf_op jit(solution)/shard_map/all_gather | solution.py:56
  141.8 3.9 fusion.16
  145.7 3.2 fusion.102
  149.2 7.0 %fusion.86 = (bf16[2,1024,512]{2,1,0:T(8,128)(2,1)}, f32[2,1024,512]{2,1,0:T(8,128)}) fusion(f32[2,1024,512]{2,1,0:T(8,128)S(1)} %copy-done.2, f32[1,1024,512]{2,1,0:T(8,128)S(1)} %bitcast.73, f32[1,1024,512]{2,1,0:T(8,128)S(1)} %bitcast.71, f32[1,2,1024,512]{3,2,1,0:T(8,128)} %param.14), kind=kLoop, calls=%fused_computation.144 | loop fusion | flops 6291456 | bytes 18874368 | tf_op jit(solution)/shard_map/convert_element_type | solution.py:39
  156.2 3.4 collective-permute-start
  159.7 2.8 gather_fusion.2
  162.5 20.5 %collective-permute-done = bf16[2,1024,512]{2,1,0:T(8,128)(2,1)S(1)} collective-permute-done((bf16[2,1024,512]{2,1,0:T(8,128)(2,1)}, bf16[2,1024,512]{2,1,0:T(8,128)(2,1)S(1)}, u32[]{:S(2)}, u32[]{:S(2)}) %collective-permute-start) | collective-permute-done | bytes 2097184 | tf_op jit(solution)/shard_map/ppermute | solution.py:15
  183.0 5.5 fusion.9
  188.5 0.8 fusion.36
  189.3 0.6 copy-done.15
  189.8 1.0 copy-done.21
  190.8 1.8 convolution_convert_fusion.1
  192.8 0.7 gather_fusion.3
  193.5 69.1 %reduce-scatter.7.cloned.1.call-done = bf16[64,1024]{1,0:T(8,128)(2,1)} async-done(((bf16[512,1024]{1,0:T(8,128)(2,1)}), bf16[64,1024]{1,0:T(8,128)(2,1)}) %reduce-scatter.7.cloned.1.call-update) | async-done | bytes 131088 | tf_op jit(solution)/shard_map/reduce_scatter | solution.py:52
  262.5 1.7 multiply_convert_fusion.4
  264.5 45.9 %all-gather.7.cloned.1.call-done = bf16[512,1024]{1,0:T(8,128)(2,1)} async-done(((bf16[64,1024]{1,0:T(8,128)(2,1)}), bf16[512,1024]{1,0:T(8,128)(2,1)}) %all-gather.7.cloned.1.call-update) | async-done | bytes 1048592 | tf_op jit(solution)/shard_map/all_gather | solution.py:56
  310.4 3.9 fusion.15
  314.3 2.5 fusion.103
  317.1 5.2 fusion.105
  322.3 1.3 collective-permute-start.1
  323.6 2.8 gather_fusion.4
  326.4 43.2 %collective-permute-done.1 = bf16[2,1024,512]{2,1,0:T(8,128)(2,1)} collective-permute-done((bf16[2,1024,512]{2,1,0:T(8,128)(2,1)}, bf16[2,1024,512]{2,1,0:T(8,128)(2,1)}, u32[]{:S(2)}, u32[]{:S(2)}) %collective-permute-start.1) | collective-permute-done | bytes 2097184 | tf_op jit(solution)/shard_map/ppermute | solution.py:15
  369.7 6.3 %fusion.10 = bf16[2,1024,512]{2,1,0:T(8,128)(2,1)S(1)} fusion(bf16[2,1024,512]{2,1,0:T(8,128)(2,1)} %collective-permute-done.1, f32[1,1024,512]{2,1,0:T(8,128)} %bitcast.68, f32[1,1024,512]{2,1,0:T(8,128)S(1)} %bitcast.64, f32[2,1024,512]{2,1,0:T(8,128)} %get-tuple-element.12, bf16[2,1024,512]{2,1,0:T(8,128)(2,1)} %copy-done.6, f32[2,1024,512]{2,1,0:T(8,128)} %param.13), kind=kLoop, calls=%fused_computation.26 | loop fusion | flops 14680064 | bytes 18874368 | tf_op jit(solution)/shard_map/convert_element_type | solution.py:45
  376.0 0.8 fusion.35
  376.7 0.6 copy-done.14
  377.3 1.0 copy-done.20
  378.3 1.8 convolution_convert_fusion
  380.2 0.7 gather_fusion.5
  380.9 68.4 %reduce-scatter.9.cloned.1.call-done = bf16[64,1024]{1,0:T(8,128)(2,1)} async-done(((bf16[512,1024]{1,0:T(8,128)(2,1)}), bf16[64,1024]{1,0:T(8,128)(2,1)}) %reduce-scatter.9.cloned.1.call-update) | async-done | bytes 131088 | tf_op jit(solution)/shard_map/reduce_scatter | solution.py:52
  449.3 1.7 multiply_convert_fusion.3
  451.1 46.2 %all-gather.9.cloned.1.call-done = bf16[512,1024]{1,0:T(8,128)(2,1)} async-done(((bf16[64,1024]{1,0:T(8,128)(2,1)}), bf16[512,1024]{1,0:T(8,128)(2,1)}) %all-gather.9.cloned.1.call-update) | async-done | bytes 1048592 | tf_op jit(solution)/shard_map/all_gather | solution.py:56
  497.3 5.3 fusion.14
  502.6 2.2 fusion.104
  504.9 1.3 copy-done.12
  506.2 6.9 %fusion.4 = bf16[2,1024,512]{2,1,0:T(8,128)(2,1)} fusion(f32[2,1024,512]{2,1,0:T(8,128)S(1)} %copy-done.4, f32[1,1024,512]{2,1,0:T(8,128)S(1)} %bitcast.77, f32[1,1024,512]{2,1,0:T(8,128)} %bitcast.75, bf16[2,1024,512]{2,1,0:T(8,128)(2,1)} %collective-permute-done.1, f32[1,1024,512]{2,1,0:T(8,128)} %bitcast.69, f32[1,1024,512]{2,1,0:T(8,128)S(1)} %bitcast.65, ...), kind=kLoop, calls=%fused_computation.13 | loop fusion | flops 22020096 | bytes 23068672 | tf_op jit(solution)/shard_map/convert_element_type | solution.py:69
  513.4 60.7 %reduce-scatter.11.cloned.1.call-done = bf16[2,64,512]{2,1,0:T(8,128)(2,1)} async-done(((bf16[2,1024,512]{2,1,0:T(8,128)(2,1)}), bf16[2,64,512]{2,1,0:T(8,128)(2,1)}) %reduce-scatter.11.cloned.1.call-update) | async-done | bytes 131088 | tf_op jit(solution)/shard_map/reduce_scatter | solution.py:70
  574.1 7.7 %fusion.8 = f32[1,2,1024,512]{3,2,1,0:T(8,128)} fusion(f32[1,1,1024,512]{3,2,1,0:T(8,128)} %bitcast.74, f32[1,1,1024,512]{3,2,1,0:T(8,128)} %bitcast.72, f32[1,1,1024,512]{3,2,1,0:T(8,128)} %bitcast.70, f32[1,1,1024,512]{3,2,1,0:T(8,128)S(1)} %bitcast.66, f32[1,1,1024,512]{3,2,1,0:T(8,128)} %bitcast.78, f32[1,1,1024,512]{3,2,1,0:T(8,128)} %bitcast.76, ...), kind=kLoop, calls=%fused_computation.18 | loop fusion | flops 9437184 | bytes 20971520 | tf_op jit(solution)/shard_map/add | solution.py:66
  581.8 30.7 %all-gather.11.cloned.1.call-done = bf16[2,1024,512]{2,1,0:T(8,128)(2,1)} async-done(((bf16[2,64,512]{2,1,0:T(8,128)(2,1)}), bf16[2,1024,512]{2,1,0:T(8,128)(2,1)}) %all-gather.11.cloned.1.call-update) | async-done | bytes 2097168 | tf_op jit(solution)/shard_map/all_gather | solution.py:71
  612.5 9.0 %multiply_subtract_fusion = (f32[2,1024,512]{2,1,0:T(8,128)}, f32[2,1024,512]{2,1,0:T(8,128)}) fusion(f32[2,1024,512]{2,1,0:T(8,128)} %param.13, bf16[2,1024,512]{2,1,0:T(8,128)(2,1)} %all-gather.11.cloned.1.call-done, f32[2,1024,512]{2,1,0:T(8,128)} %param.15), kind=kLoop, calls=%fused_computation.19 | loop fusion | flops 6291456 | bytes 18874368 | tf_op jit(solution)/shard_map/sub | solution.py:73
  (69 shorter events, 1.9 us)
Async XLA Ops:
  7.2 3.4 copy-start
  7.2 86.0 %reduce-scatter.5.cloned.1.call-start = ((), (), s32[]{:S(2)}) async-start(), calls=%async_computation.4 | async-start | bytes 1179648 | tf_op jit(solution)/shard_map/reduce_scatter | solution.py:52
  10.5 2.8 copy-start.13
  15.3 1.0 copy-start.19
  16.3 3.3 copy-start.7
  19.4 122.3 %all-gather.5.cloned.1.call-start = ((), (), s32[]{:S(2)}) async-start(), calls=%async_computation.5 | async-start | bytes 1179648 | tf_op jit(solution)/shard_map/all_gather | solution.py:56
  94.9 167.6 %reduce-scatter.7.cloned.1.call-start = ((), (), s32[]{:S(2)}) async-start(), calls=%async_computation.6 | async-start | bytes 1179648 | tf_op jit(solution)/shard_map/reduce_scatter | solution.py:52
  145.7 10.6 %copy-start.10 = (f32[1024,512]{1,0:T(8,128)}, f32[1024,512]{1,0:T(8,128)S(1)}, u32[]{:S(2)}) copy-start(f32[1024,512]{1,0:T(8,128)S(1)} %fusion.16) | copy-start | bytes 6291460
  145.7 3.6 copy-start.2
  148.9 7.3 %copy-start.11 = (f32[1024,512]{1,0:T(8,128)}, f32[1024,512]{1,0:T(8,128)S(1)}, u32[]{:S(2)}) copy-start(f32[1024,512]{1,0:T(8,128)S(1)} %fusion.102) | copy-start | bytes 6291460
  156.2 26.7 %collective-permute-start = (bf16[2,1024,512]{2,1,0:T(8,128)(2,1)}, bf16[2,1024,512]{2,1,0:T(8,128)(2,1)S(1)}, u32[]{:S(2)}, u32[]{:S(2)}) collective-permute-start(bf16[2,1024,512]{2,1,0:T(8,128)(2,1)} %get-tuple-element.11), channel_id=1, source_target_pairs={{120,0},{0,8},{8,16},{16,24},{24,32},{32,40},{40,48},{48,56},{56,6... | collective-permute-start | bytes 6291464 | tf_op jit(solution)/shard_map/ppermute | solution.py:15
  183.0 5.5 copy-start.6
  183.0 5.5 copy-start.16
  188.5 1.3 copy-start.15
  189.8 1.0 copy-start.21
  190.8 1.9 copy-start.8
  192.6 117.8 %all-gather.7.cloned.1.call-start = ((), (), s32[]{:S(2)}) async-start(), calls=%async_computation.7 | async-start | bytes 1179648 | tf_op jit(solution)/shard_map/all_gather | solution.py:56
  264.2 185.1 %reduce-scatter.9.cloned.1.call-start = ((), (), s32[]{:S(2)}) async-start(), calls=%async_computation.8 | async-start | bytes 1179648 | tf_op jit(solution)/shard_map/reduce_scatter | solution.py:52
  314.3 2.8 copy-start.3
  316.9 5.4 copy-start.5
  322.3 47.3 %collective-permute-start.1 = (bf16[2,1024,512]{2,1,0:T(8,128)(2,1)}, bf16[2,1024,512]{2,1,0:T(8,128)(2,1)}, u32[]{:S(2)}, u32[]{:S(2)}) collective-permute-start(bf16[2,1024,512]{2,1,0:T(8,128)(2,1)} %fusion.105), channel_id=1, source_target_pairs={{112,0},{120,8},{0,16},{8,24},{16,32},{24,40},{32,48},{40,56},{48,... | collective-permute-start | bytes 6291464 | tf_op jit(solution)/shard_map/ppermute | solution.py:15
  326.4 49.5 %copy-start.17 = (bf16[512,1024]{1,0:T(8,128)(2,1)S(1)}, bf16[512,1024]{1,0:T(8,128)(2,1)}, u32[]{:S(2)}) copy-start(bf16[512,1024]{1,0:T(8,128)(2,1)} %gather_fusion.4) | copy-start | bytes 3145732
  376.0 1.3 copy-start.14
  377.3 1.0 copy-start.20
  378.3 1.9 copy-start.9
  380.1 117.2 %all-gather.9.cloned.1.call-start = ((), (), s32[]{:S(2)}) async-start(), calls=%async_computation.9 | async-start | bytes 1179648 | tf_op jit(solution)/shard_map/all_gather | solution.py:56
  451.0 123.1 %reduce-scatter.11.cloned.1.call-start = ((), (), s32[]{:S(2)}) async-start(), calls=%async_computation.10 | async-start | bytes 2228224 | tf_op jit(solution)/shard_map/reduce_scatter | solution.py:70
  497.2 5.3 copy-start.18
  502.6 3.6 copy-start.4
  504.8 1.3 copy-start.12
  513.1 99.4 %all-gather.11.cloned.1.call-start = ((), (), s32[]{:S(2)}) async-start(), calls=%async_computation.11 | async-start | bytes 2228224 | tf_op jit(solution)/shard_map/all_gather | solution.py:71
  612.5 9.0 %copy-start.1 = (bf16[512,1024]{1,0:T(8,128)(2,1)S(1)}, bf16[512,1024]{1,0:T(8,128)(2,1)}, u32[]{:S(2)}) copy-start(bf16[512,1024]{1,0:T(8,128)(2,1)} %param.10) | copy-start | bytes 3145732
Sparse Core Ops, SparseCore 0:
  19.5 73.6 reduce-scatter.4
  96.1 45.5 all-gather.4
  192.7 69.7 reduce-scatter.6
  264.8 45.6 all-gather.6
  380.2 69.1 reduce-scatter.8
  451.6 45.6 all-gather.8
  513.2 60.8 reduce-scatter.10
  575.8 36.6 all-gather.10
where the time goes:
time: 629 us; the launch traced here: 628 us
  waiting for transfers between devices  505 us (80%)
  other arithmetic  55.4 us (9%)
  matrix products  31.2 us (5%)
  local copies, waits for them, and re-layouts  17.4 us (3%)
  between operations  14.4 us (2%)
    reduce_scatter x3, waiting for transfers between devices, body(): lax.psum_scatter(partial_out, 'tensor', scatter_dimension=0, tiled=True)  210 us
    all_gather x3, waiting for transfers between devices, body(): error = lax.all_gather(error, 'tensor', axis=0, tiled=True)  139 us
    ppermute x2, waiting for transfers between devices, passed_along(): return lax.ppermute(block, axis, route)  63.7 us
    reduce_scatter x1, waiting for transfers between devices, body(): total = lax.psum_scatter(moved, 'replica', scatter_dimension=1, tiled=True)  60.7 us
    all_gather x1, waiting for transfers between devices, body(): total = lax.all_gather(total, 'replica', axis=1, tiled=True)  30.7 us
    convert_element_type x3, other arithmetic, body(): weights_bf = weights.astype(jnp.bfloat16)  14.2 us
    dot_general x3, matrix products, body(): lax.dot_general(inputs, back, (((0,), (0,)), ((), ())), preferred_element...  13.1 us
  transfers between devices with their start and end apart: 10, of which 10 were waited for; matrix products, arithmetic and copies ran while one was open for 2% of the time, Pallas kernels for 0%

commit v1 on v0

--- a/solution.py
+++ b/solution.py
@@ -53,7 +53,9 @@
         error = ((summed.astype(jnp.float32) - wanted.astype(jnp.float32)) * scale).astype(
             jnp.bfloat16
         )
-        error = lax.all_gather(error, "tensor", axis=0, tiled=True)
+        error = jnp.concatenate(
+            lax.all_to_all(jnp.stack([error] * lax.axis_size("tensor")), "tensor", 0, 0), axis=0
+        )
         back = (jnp.dot(error, weights_bf[1], preferred_element_type=jnp.float32) * slope).astype(
             jnp.bfloat16
         )

time: 629 us -> 543 us (0.86)
  waiting for transfers between devices: 505 us -> 363 us
  blocking collectives: 0 us -> 56.9 us
    all_gather x3 -> x0, waiting for transfers between devices: 139 us -> none  [body(): error = lax.all_gather(error, 'tensor', axis=0, tiled=True)]
    all_to_all x0 -> x3, blocking collectives: none -> 56.9 us  [body(): lax.all_to_all(jnp.stack([error] * lax.axis_size('tensor')), 'tensor', 0, 0)]
  transfers between devices with their start and end apart: 10 -> 7, of which waited for: 10 -> 7; matrix products, arithmetic and copies ran while one was open for 2% -> 3% of each run, Pallas kernels for 0% -> 0%
where the time goes in v1:
time: 543 us
  waiting for transfers between devices  363 us (67%)
  blocking collectives  56.9 us (10%)
  other arithmetic  53.4 us (10%)
  matrix products  31.3 us (6%)
  local copies, waits for them, and re-layouts  17.7 us (3%)
  between operations  14.1 us (3%)
  starting transfers between devices  6.46 us (1%)
    reduce_scatter x3, waiting for transfers between devices, body(): lax.psum_scatter(partial_out, 'tensor', scatter_dimension=0, tiled=True)  210 us
    ppermute x2, waiting for transfers between devices, passed_along(): return lax.ppermute(block, axis, route)  62.4 us
    reduce_scatter x1, waiting for transfers between devices, body(): total = lax.psum_scatter(moved, 'replica', scatter_dimension=1, tiled=True)  60.7 us
    all_to_all x3, blocking collectives, body(): lax.all_to_all(jnp.stack([error] * lax.axis_size('tensor')), 'tensor', 0, 0)  56.9 us
    all_gather x1, waiting for transfers between devices, body(): total = lax.all_gather(total, 'replica', axis=1, tiled=True)  30.1 us
    convert_element_type x3, other arithmetic, body(): weights_bf = weights.astype(jnp.bfloat16)  14.2 us
    dot_general x3, matrix products, body(): lax.dot_general(inputs, back, (((0,), (0,)), ((), ())), preferred_element...  13.1 us
    convert_element_type x2, other arithmetic, body(): weights.astype(jnp.bfloat16)  12.2 us
  transfers between devices with their start and end apart: 7, of which 7 were waited for; matrix products, arithmetic and copies ran while one was open for 3% of the time, Pallas kernels for 0%

profile of v1, /device:TPU:1, one launch (start us, length us, event | category | flops | bytes accessed | tf_op | source)
XLA Modules:
  0.0 543.0 jit_solution(10677576147503099453)
XLA Ops:
  7.2 0.8 fusion.106
  8.1 2.5 convert_element_type.81
  10.5 2.8 gather_fusion
  13.3 2.0 fusion.37
  15.3 1.0 copy-done.19
  16.3 3.1 convolution_convert_fusion.2
  19.6 0.7 gather_fusion.1
  20.3 72.9 %reduce-scatter.5.cloned.1.call-done = bf16[64,1024]{1,0:T(8,128)(2,1)} async-done(((bf16[512,1024]{1,0:T(8,128)(2,1)}), bf16[64,1024]{1,0:T(8,128)(2,1)}) %reduce-scatter.5.cloned.1.call-update) | async-done | bytes 131088 | tf_op jit(solution)/shard_map/reduce_scatter | solution.py:52
  93.2 1.0 multiply_convert_fusion.5
  94.3 19.0 %all_to_all.15 = bf16[8,64,1024]{2,1,0:T(8,128)(2,1)} all-to-all(bf16[8,64,1024]{2,1,0:T(8,128)(2,1)S(1)} %stack.78), channel_id=1, replica_groups=mesh['replica'=16,'tensor'=8] {'tensor'}, dimensions={0} | all-to-all | bytes 2097152 | tf_op jit(solution)/shard_map/all_to_all | solution.py:57
  113.3 3.9 fusion.16
  117.2 3.2 fusion.102
  120.8 7.0 %fusion.86 = (bf16[2,1024,512]{2,1,0:T(8,128)(2,1)}, f32[2,1024,512]{2,1,0:T(8,128)}) fusion(f32[2,1024,512]{2,1,0:T(8,128)S(1)} %copy-done.2, f32[1,1024,512]{2,1,0:T(8,128)S(1)} %bitcast.76, f32[1,1024,512]{2,1,0:T(8,128)S(1)} %bitcast.74, f32[1,2,1024,512]{3,2,1,0:T(8,128)} %param.14), kind=kLoop, calls=%fused_computation.144 | loop fusion | flops 6291456 | bytes 18874368 | tf_op jit(solution)/shard_map/convert_element_type | solution.py:39
  127.8 4.7 collective-permute-start
  132.5 2.8 gather_fusion.2
  135.3 20.5 %collective-permute-done = bf16[2,1024,512]{2,1,0:T(8,128)(2,1)S(1)} collective-permute-done((bf16[2,1024,512]{2,1,0:T(8,128)(2,1)}, bf16[2,1024,512]{2,1,0:T(8,128)(2,1)S(1)}, u32[]{:S(2)}, u32[]{:S(2)}) %collective-permute-start) | collective-permute-done | bytes 2097184 | tf_op jit(solution)/shard_map/ppermute | solution.py:15
  155.8 5.5 %fusion.9 = bf16[2,1024,512]{2,1,0:T(8,128)(2,1)S(1)} fusion(bf16[2,1024,512]{2,1,0:T(8,128)(2,1)S(1)} %collective-permute-done, f32[2,1024,512]{2,1,0:T(8,128)} %param.13, f32[2,1024,512]{2,1,0:T(8,128)} %get-tuple-element.12), kind=kLoop, calls=%fused_computation.25 | loop fusion | flops 6291456 | bytes 12582912 | tf_op jit(solution)/shard_map/convert_element_type | solution.py:45
  161.3 0.8 fusion.36
  162.1 0.6 copy-done.15
  162.6 1.0 copy-done.21
  163.6 1.8 convolution_convert_fusion.1
  165.6 0.7 gather_fusion.3
  166.3 67.6 %reduce-scatter.7.cloned.1.call-done = bf16[64,1024]{1,0:T(8,128)(2,1)} async-done(((bf16[512,1024]{1,0:T(8,128)(2,1)}), bf16[64,1024]{1,0:T(8,128)(2,1)}) %reduce-scatter.7.cloned.1.call-update) | async-done | bytes 131088 | tf_op jit(solution)/shard_map/reduce_scatter | solution.py:52
  233.9 1.0 multiply_convert_fusion.4
  235.0 19.0 %all_to_all.16 = bf16[8,64,1024]{2,1,0:T(8,128)(2,1)} all-to-all(bf16[8,64,1024]{2,1,0:T(8,128)(2,1)S(1)} %stack.82), channel_id=1, replica_groups=mesh['replica'=16,'tensor'=8] {'tensor'}, dimensions={0} | all-to-all | bytes 2097152 | tf_op jit(solution)/shard_map/all_to_all | solution.py:57
  254.0 3.9 fusion.15
  257.9 2.5 fusion.103
  260.7 5.2 fusion.105
  265.9 1.3 collective-permute-start.1
  267.2 2.8 gather_fusion.4
  270.1 41.9 %collective-permute-done.1 = bf16[2,1024,512]{2,1,0:T(8,128)(2,1)} collective-permute-done((bf16[2,1024,512]{2,1,0:T(8,128)(2,1)}, bf16[2,1024,512]{2,1,0:T(8,128)(2,1)}, u32[]{:S(2)}, u32[]{:S(2)}) %collective-permute-start.1) | collective-permute-done | bytes 2097184 | tf_op jit(solution)/shard_map/ppermute | solution.py:15
  312.0 6.3 %fusion.10 = bf16[2,1024,512]{2,1,0:T(8,128)(2,1)S(1)} fusion(bf16[2,1024,512]{2,1,0:T(8,128)(2,1)} %collective-permute-done.1, f32[1,1024,512]{2,1,0:T(8,128)} %bitcast.71, f32[1,1024,512]{2,1,0:T(8,128)S(1)} %bitcast.67, f32[2,1024,512]{2,1,0:T(8,128)} %get-tuple-element.12, bf16[2,1024,512]{2,1,0:T(8,128)(2,1)} %copy-done.6, f32[2,1024,512]{2,1,0:T(8,128)} %param.13), kind=kLoop, calls=%fused_computation.26 | loop fusion | flops 14680064 | bytes 18874368 | tf_op jit(solution)/shard_map/convert_element_type | solution.py:45
  318.3 0.8 fusion.35
  319.0 0.6 copy-done.14
  319.6 1.0 copy-done.20
  320.6 1.8 convolution_convert_fusion
  322.6 0.7 gather_fusion.5
  323.3 69.4 %reduce-scatter.9.cloned.1.call-done = bf16[64,1024]{1,0:T(8,128)(2,1)} async-done(((bf16[512,1024]{1,0:T(8,128)(2,1)}), bf16[64,1024]{1,0:T(8,128)(2,1)}) %reduce-scatter.9.cloned.1.call-update) | async-done | bytes 131088 | tf_op jit(solution)/shard_map/reduce_scatter | solution.py:52
  392.7 1.0 multiply_convert_fusion.3
  393.9 19.0 %all_to_all.17 = bf16[8,64,1024]{2,1,0:T(8,128)(2,1)} all-to-all(bf16[8,64,1024]{2,1,0:T(8,128)(2,1)S(1)} %stack.86), channel_id=1, replica_groups=mesh['replica'=16,'tensor'=8] {'tensor'}, dimensions={0} | all-to-all | bytes 2097152 | tf_op jit(solution)/shard_map/all_to_all | solution.py:57
  412.9 5.3 fusion.14
  418.2 2.2 fusion.104
  420.4 1.3 copy-done.12
  421.8 6.9 %fusion.4 = bf16[2,1024,512]{2,1,0:T(8,128)(2,1)} fusion(f32[2,1024,512]{2,1,0:T(8,128)S(1)} %copy-done.4, f32[1,1024,512]{2,1,0:T(8,128)S(1)} %bitcast.80, f32[1,1024,512]{2,1,0:T(8,128)} %bitcast.78, bf16[2,1024,512]{2,1,0:T(8,128)(2,1)} %collective-permute-done.1, f32[1,1024,512]{2,1,0:T(8,128)} %bitcast.72, f32[1,1024,512]{2,1,0:T(8,128)S(1)} %bitcast.68, ...), kind=kLoop, calls=%fused_computation.13 | loop fusion | flops 22020096 | bytes 23068672 | tf_op jit(solution)/shard_map/convert_element_type | solution.py:71
  428.9 60.7 %reduce-scatter.11.cloned.1.call-done = bf16[2,64,512]{2,1,0:T(8,128)(2,1)} async-done(((bf16[2,1024,512]{2,1,0:T(8,128)(2,1)}), bf16[2,64,512]{2,1,0:T(8,128)(2,1)}) %reduce-scatter.11.cloned.1.call-update) | async-done | bytes 131088 | tf_op jit(solution)/shard_map/reduce_scatter | solution.py:72
  489.7 7.7 %fusion.8 = f32[1,2,1024,512]{3,2,1,0:T(8,128)} fusion(f32[1,1,1024,512]{3,2,1,0:T(8,128)} %bitcast.77, f32[1,1,1024,512]{3,2,1,0:T(8,128)} %bitcast.75, f32[1,1,1024,512]{3,2,1,0:T(8,128)} %bitcast.73, f32[1,1,1024,512]{3,2,1,0:T(8,128)S(1)} %bitcast.69, f32[1,1,1024,512]{3,2,1,0:T(8,128)} %bitcast.81, f32[1,1,1024,512]{3,2,1,0:T(8,128)} %bitcast.79, ...), kind=kLoop, calls=%fused_computation.18 | loop fusion | flops 9437184 | bytes 20971520 | tf_op jit(solution)/shard_map/add | solution.py:68
  497.3 30.1 %all-gather.2.cloned.1.call-done = bf16[2,1024,512]{2,1,0:T(8,128)(2,1)} async-done(((bf16[2,64,512]{2,1,0:T(8,128)(2,1)}), bf16[2,1024,512]{2,1,0:T(8,128)(2,1)}) %all-gather.2.cloned.1.call-update) | async-done | bytes 2097168 | tf_op jit(solution)/shard_map/all_gather | solution.py:73
  527.5 9.0 %multiply_subtract_fusion = (f32[2,1024,512]{2,1,0:T(8,128)}, f32[2,1024,512]{2,1,0:T(8,128)}) fusion(f32[2,1024,512]{2,1,0:T(8,128)} %param.13, bf16[2,1024,512]{2,1,0:T(8,128)(2,1)} %all-gather.2.cloned.1.call-done, f32[2,1024,512]{2,1,0:T(8,128)} %param.15), kind=kLoop, calls=%fused_computation.19 | loop fusion | flops 6291456 | bytes 18874368 | tf_op jit(solution)/shard_map/sub | solution.py:75
  (66 shorter events, 1.9 us)
Async XLA Ops:
  7.2 3.4 copy-start
  7.2 86.0 %reduce-scatter.5.cloned.1.call-start = ((), (), s32[]{:S(2)}) async-start(), calls=%async_computation.7 | async-start | bytes 1179648 | tf_op jit(solution)/shard_map/reduce_scatter | solution.py:52
  10.5 2.8 copy-start.13
  15.3 1.0 copy-start.19
  16.3 3.3 copy-start.7
  19.4 214.5 %reduce-scatter.7.cloned.1.call-start = ((), (), s32[]{:S(2)}) async-start(), calls=%async_computation.8 | async-start | bytes 1179648 | tf_op jit(solution)/shard_map/reduce_scatter | solution.py:52
  117.2 10.6 %copy-start.10 = (f32[1024,512]{1,0:T(8,128)}, f32[1024,512]{1,0:T(8,128)S(1)}, u32[]{:S(2)}) copy-start(f32[1024,512]{1,0:T(8,128)S(1)} %fusion.16) | copy-start | bytes 6291460
  117.2 3.6 copy-start.2
  120.4 7.3 %copy-start.11 = (f32[1024,512]{1,0:T(8,128)}, f32[1024,512]{1,0:T(8,128)S(1)}, u32[]{:S(2)}) copy-start(f32[1024,512]{1,0:T(8,128)S(1)} %fusion.102) | copy-start | bytes 6291460
  127.8 28.0 %collective-permute-start = (bf16[2,1024,512]{2,1,0:T(8,128)(2,1)}, bf16[2,1024,512]{2,1,0:T(8,128)(2,1)S(1)}, u32[]{:S(2)}, u32[]{:S(2)}) collective-permute-start(bf16[2,1024,512]{2,1,0:T(8,128)(2,1)} %get-tuple-element.11), channel_id=1, source_target_pairs={{120,0},{0,8},{8,16},{16,24},{24,32},{32,40},{40,48},{48,56},{56,6... | collective-permute-start | bytes 6291464 | tf_op jit(solution)/shard_map/ppermute | solution.py:15
  155.8 5.5 %copy-start.6 = (bf16[2,1024,512]{2,1,0:T(8,128)(2,1)}, bf16[2,1024,512]{2,1,0:T(8,128)(2,1)S(1)}, u32[]{:S(2)}) copy-start(bf16[2,1024,512]{2,1,0:T(8,128)(2,1)S(1)} %collective-permute-done) | copy-start | bytes 6291460
  155.8 5.5 %copy-start.16 = (bf16[512,1024]{1,0:T(8,128)(2,1)S(1)}, bf16[512,1024]{1,0:T(8,128)(2,1)}, u32[]{:S(2)}) copy-start(bf16[512,1024]{1,0:T(8,128)(2,1)} %gather_fusion.2) | copy-start | bytes 3145732
  161.3 1.3 copy-start.15
  162.6 1.0 copy-start.21
  163.6 1.9 copy-start.8
  165.4 227.3 %reduce-scatter.9.cloned.1.call-start = ((), (), s32[]{:S(2)}) async-start(), calls=%async_computation.9 | async-start | bytes 1179648 | tf_op jit(solution)/shard_map/reduce_scatter | solution.py:52
  257.9 2.8 copy-start.3
  260.4 5.4 %copy-start.5 = (f32[1024,512]{1,0:T(8,128)}, f32[1024,512]{1,0:T(8,128)S(1)}, u32[]{:S(2)}) copy-start(f32[1024,512]{1,0:T(8,128)S(1)} %fusion.103) | copy-start | bytes 6291460
  265.9 46.1 %collective-permute-start.1 = (bf16[2,1024,512]{2,1,0:T(8,128)(2,1)}, bf16[2,1024,512]{2,1,0:T(8,128)(2,1)}, u32[]{:S(2)}, u32[]{:S(2)}) collective-permute-start(bf16[2,1024,512]{2,1,0:T(8,128)(2,1)} %fusion.105), channel_id=1, source_target_pairs={{112,0},{120,8},{0,16},{8,24},{16,32},{24,40},{32,48},{40,56},{48,... | collective-permute-start | bytes 6291464 | tf_op jit(solution)/shard_map/ppermute | solution.py:15
  270.1 48.2 %copy-start.17 = (bf16[512,1024]{1,0:T(8,128)(2,1)S(1)}, bf16[512,1024]{1,0:T(8,128)(2,1)}, u32[]{:S(2)}) copy-start(bf16[512,1024]{1,0:T(8,128)(2,1)} %gather_fusion.4) | copy-start | bytes 3145732
  318.3 1.3 copy-start.14
  319.6 1.0 copy-start.20
  320.6 2.0 copy-start.9
  322.4 167.2 %reduce-scatter.11.cloned.1.call-start = ((), (), s32[]{:S(2)}) async-start(), calls=%async_computation.10 | async-start | bytes 2228224 | tf_op jit(solution)/shard_map/reduce_scatter | solution.py:72
  412.8 5.3 copy-start.18
  418.2 3.6 copy-start.4
  420.4 1.3 copy-start.12
  428.7 98.8 %all-gather.2.cloned.1.call-start = ((), (), s32[]{:S(2)}) async-start(), calls=%async_computation.11 | async-start | bytes 2228224 | tf_op jit(solution)/shard_map/all_gather | solution.py:73
  527.5 9.0 %copy-start.1 = (bf16[512,1024]{1,0:T(8,128)(2,1)S(1)}, bf16[512,1024]{1,0:T(8,128)(2,1)}, u32[]{:S(2)}) copy-start(bf16[512,1024]{1,0:T(8,128)(2,1)} %param.10) | copy-start | bytes 3145732
Sparse Core Ops, SparseCore 0:
  19.5 73.6 reduce-scatter.4
  165.5 68.3 reduce-scatter.6
  322.5 70.1 reduce-scatter.8
  428.8 60.7 reduce-scatter.10
  491.1 36.2 all-gather.1
